TPU v7x, 32 devices: a whole 2x2x4 slice. The times are simulated.
32 devices in a mesh: ep: 16 (over z, x, core), fs: 2 (over y).
Axes of the slice: x: 2, y: 2, z: 4, core: 2. Of those that a mesh axis runs over, the one named last changes fastest.
Arguments:
- tokens: bfloat16 [2048, 4096], P('ep', 'fs'), may hold values from -6 to 6
- cotangent: bfloat16 [2048, 4096], P('ep', 'fs'), may hold values from -3 to 3
- gate_probs: bfloat16 [2048, 8], P('ep'), may hold values from 0.019897461 to 0.3984375
- expert_ids: int32 [2048, 8], P('ep'), may hold values from 0 to 15, all different within a row; in each aligned block of 128 rows (0 to 127, 128 to 255, ...) at most 72 rows name the same one
- w_gate: bfloat16 [16, 4096, 768], P('ep', 'fs'), may hold values from -0.09375 to 0.09375
- w_up: bfloat16 [16, 4096, 768], P('ep', 'fs'), may hold values from -0.09375 to 0.09375
- w_down: bfloat16 [16, 768, 4096], P('ep', None, 'fs'), may hold values from -0.21875 to 0.21875
Outputs:
- grad_tokens: bfloat16 [2048, 4096], P('ep', 'fs')
- grad_probs: bfloat16 [2048, 8], P('ep')
- grad_w_gate: bfloat16 [16, 4096, 768], P('ep', 'fs')
- grad_w_up: bfloat16 [16, 4096, 768], P('ep', 'fs')
- grad_w_down: bfloat16 [16, 768, 4096], P('ep', None, 'fs')
Inputs may be any that keep to these rules, and one draw needn't show every extreme that they name: `expert_ids`: each token names 8 different experts. Among the 128 tokens of one index of ep, no expert is named by more than 72 of them, and in every draw some expert is named by exactly 72.
All inputs are finite; a program needn't handle non-finite values.
Results may differ from a plain program's by a relative error of at most 0.025.
Values may be sent and summed in bfloat16 or wider, within the bound.
A program may use at most 128 MiB of HBM per device.

v0:
```python
import jax
import jax.numpy as jnp
from jax import lax
from jax.sharding import PartitionSpec as P


def build_slots(routing, experts, capacity):
    flat_ids = routing.reshape(-1)
    choose = (flat_ids[:, None] == jnp.arange(experts, dtype=jnp.int32)[None, :]).astype(jnp.int32)
    earlier = jnp.cumsum(choose, axis=0) - choose
    position = jnp.sum(earlier * choose, axis=1)
    slot_of = flat_ids * capacity + position
    pair_number = jnp.arange(flat_ids.shape[0], dtype=jnp.int32) + 1
    filled_by = jnp.zeros((experts * capacity,), jnp.int32).at[slot_of].set(pair_number)
    return (slot_of, filled_by)


def activate(gate_up, hidden_units):
    gate_proj = gate_up[:, :hidden_units].astype(jnp.float32)
    up_proj = gate_up[:, hidden_units:].astype(jnp.float32)
    sigmoid_gate = jax.nn.sigmoid(gate_proj)
    gate_act = gate_proj * sigmoid_gate
    return (gate_proj, up_proj, sigmoid_gate, gate_act)


def local_grads(raw_grad, gate_up, prob_rows, hidden_units):
    gate_proj, up_proj, sigmoid_gate, gate_act = activate(gate_up, hidden_units)
    hidden = (gate_act * up_proj).astype(jnp.bfloat16)
    scaled = prob_rows.astype(jnp.float32)[:, None] * raw_grad
    grad_gate = scaled * up_proj * sigmoid_gate * (1.0 + gate_proj * (1.0 - sigmoid_gate))
    grad_up = scaled * gate_act
    grad_gate_up = jnp.concatenate(
        [grad_gate.astype(jnp.bfloat16), grad_up.astype(jnp.bfloat16)], axis=1
    )
    grad_prob = jnp.sum(hidden.astype(jnp.float32) * raw_grad, axis=1).astype(jnp.bfloat16)
    return (grad_gate_up, grad_prob)


def per_device(tokens, cotangent, gate_probs, expert_ids, w_gate, w_up, w_down):
    tok_dev, top_count = expert_ids.shape
    experts = lax.axis_size("ep")
    shards = lax.axis_size("fs")
    width_dev = tokens.shape[1]
    hidden_units = w_gate.shape[2]
    capacity = (9 * tok_dev * top_count + 8 * experts - 1) // (8 * experts)
    slot_count = experts * capacity
    share_rows = slot_count // shards
    slot_of, filled_by = build_slots(expert_ids, experts, capacity)
    filled = filled_by > 0
    assign = jnp.maximum(filled_by - 1, 0)
    source_token = assign // top_count
    token_send = jnp.where(
        filled[:, None], jnp.take(tokens, source_token, axis=0), jnp.zeros((), tokens.dtype)
    ).reshape(experts, capacity, width_dev)
    grad_send = jnp.where(
        filled[:, None], jnp.take(cotangent, source_token, axis=0), jnp.zeros((), cotangent.dtype)
    ).reshape(experts, capacity, width_dev)
    prob_send = jnp.where(
        filled, jnp.take(gate_probs.reshape(-1), assign, axis=0), jnp.zeros((), gate_probs.dtype)
    ).reshape(experts, capacity)
    token_recv = lax.all_to_all(token_send, "ep", split_axis=0, concat_axis=0, tiled=True)
    token_rows = token_recv.reshape(slot_count, width_dev)
    stacked = jnp.concatenate([w_gate[0], w_up[0]], axis=1)
    down_local = w_down[0]
    section = token_rows
    summed = lax.psum(
        jnp.dot(section, stacked, preferred_element_type=jnp.float32).astype(jnp.bfloat16), "fs"
    )
    gate_up = lax.optimization_barrier(summed)
    gate_proj, up_proj, sigmoid_gate, gate_act = activate(gate_up, hidden_units)
    hidden = (gate_act * up_proj).astype(jnp.bfloat16)
    grad_recv, prob_recv = (
        lax.all_to_all(grad_send, "ep", split_axis=0, concat_axis=0, tiled=True),
        lax.all_to_all(prob_send, "ep", split_axis=0, concat_axis=0, tiled=True),
    )
    grad_rows = grad_recv.reshape(slot_count, width_dev)
    prob_rows = prob_recv.reshape(slot_count)
    weighted = (prob_rows.astype(jnp.float32)[:, None] * grad_rows.astype(jnp.float32)).astype(
        jnp.bfloat16
    )
    across_last = (((1,), (1,)), ((), ()))
    across_first = (((0,), (0,)), ((), ()))
    section = grad_rows
    raw_share = lax.psum_scatter(
        lax.dot_general(
            section, down_local, across_last, preferred_element_type=jnp.float32
        ).astype(jnp.bfloat16),
        "fs",
        scatter_dimension=0,
        tiled=True,
    ).astype(jnp.float32)
    first_row = lax.axis_index("fs") * share_rows
    share_gate_up = lax.dynamic_slice_in_dim(gate_up, first_row, share_rows, 0)
    share_prob_rows = lax.dynamic_slice_in_dim(prob_rows, first_row, share_rows, 0)
    share_grads, share_probs = local_grads(raw_share, share_gate_up, share_prob_rows, hidden_units)
    grad_gate_up, grad_prob = (
        lax.all_gather(share_grads, "fs", axis=0, tiled=True),
        lax.all_gather(share_probs, "fs", axis=0, tiled=True),
    )
    new_down = lax.dot_general(
        hidden, weighted, across_first, preferred_element_type=jnp.float32
    ).astype(jnp.bfloat16)
    joint = lax.dot_general(
        token_rows, grad_gate_up, across_first, preferred_element_type=jnp.float32
    ).astype(jnp.bfloat16)
    new_gate = joint[:, :hidden_units]
    new_up = joint[:, hidden_units:]
    grad_part = lax.dot_general(
        grad_gate_up, stacked, across_last, preferred_element_type=jnp.float32
    ).astype(jnp.bfloat16)
    part_back, prob_back = (
        lax.all_to_all(
            grad_part.reshape(experts, capacity, width_dev),
            "ep",
            split_axis=0,
            concat_axis=0,
            tiled=True,
        ),
        lax.all_to_all(
            grad_prob.reshape(experts, capacity), "ep", split_axis=0, concat_axis=0, tiled=True
        ),
    )
    returned = jnp.take(part_back.reshape(slot_count, width_dev), slot_of, axis=0)
    grad_tokens = jnp.sum(
        returned.reshape(tok_dev, top_count, width_dev).astype(jnp.float32), axis=1
    ).astype(jnp.bfloat16)
    grad_probs = jnp.take(prob_back.reshape(slot_count), slot_of, axis=0).reshape(
        tok_dev, top_count
    )
    return (grad_tokens, grad_probs, new_gate[None], new_up[None], new_down[None])


def solution(mesh):
    return jax.shard_map(
        per_device,
        mesh=mesh,
        in_specs=(
            P("ep", "fs"),
            P("ep", "fs"),
            P("ep", None),
            P("ep", None),
            P("ep", "fs", None),
            P("ep", "fs", None),
            P("ep", None, "fs"),
        ),
        out_specs=(
            P("ep", "fs"),
            P("ep", None),
            P("ep", "fs", None),
            P("ep", "fs", None),
            P("ep", None, "fs"),
        ),
        check_vma=False,
    )
```

profile of v0, /device:TPU:11, one launch (start us, length us, event | category | flops | bytes accessed | tf_op | source)
XLA Modules:
  0.0 511.1 jit_solution(11509381439095794704)
XLA Ops:
  8.3 4.5 reduce-window.6
  13.4 4.3 scatter_custom_fusion
  18.7 7.3 %gather_fusion = bf16[1152]{0:T(1024)(128)(2,1)S(1)} fusion(bf16[1024]{0:T(1024)(128)(2,1)S(1)} %reshape.132, s32[2048]{0:T(1024)S(1)} %pad_clamp_fusion.1), kind=kCustom, calls=%fused_computation.2 | custom fusion | bytes 9216 | tf_op jit(solution)/shard_map/jit(_take)/gather | solution.py:59
  26.0 11.8 %gather_fusion.4 = bf16[1152,2048]{1,0:T(8,128)(2,1)} fusion(bf16[128,2048]{1,0:T(8,128)(2,1)} %param.9, s32[2048]{0:T(1024)S(1)} %pad_clamp_fusion), kind=kCustom, calls=%fused_computation.1.clone | custom fusion | bytes 9441792 | tf_op jit(solution)/shard_map/jit(_take)/gather | solution.py:53
  37.8 11.8 %gather_fusion.3 = bf16[1152,2048]{1,0:T(8,128)(2,1)} fusion(bf16[128,2048]{1,0:T(8,128)(2,1)} %param.10, s32[2048]{0:T(1024)S(1)} %pad_clamp_fusion), kind=kCustom, calls=%fused_computation.clone | custom fusion | bytes 9441792 | tf_op jit(solution)/shard_map/jit(_take)/gather | solution.py:56
  49.5 7.5 %select_select_fusion = (bf16[1152,2048]{1,0:T(8,128)(2,1)S(1)}, bf16[1152,2048]{1,0:T(8,128)(2,1)}) fusion(bf16[1152,2048]{1,0:T(8,128)(2,1)} %gather_fusion.4, pred[1152]{0:T(1024)(128)(4,1)S(1)} %get-tuple-element.20, pred[1152]{0:T(1024)(128)(4,1)S(1)} %get-tuple-element.19, bf16[1152,2048]{1,0:T(8,128)(2,1)} %gather_fusion.3), kind=kLoop, calls=%fused_computation.12 | loop fusion | flops 9437184 | bytes 18876672 | tf_op jit(solution)/shard_map/jit(_where)/select_n | solution.py:52
  57.0 109.9 %all_to_all.35 = bf16[16,72,2048]{2,1,0:T(8,128)(2,1)} all-to-all(bf16[16,72,2048]{2,1,0:T(8,128)(2,1)S(1)} %bitcast.49), channel_id=1, replica_groups=mesh['ep'=16,'fs'=2] {'ep'}, dimensions={0} | all-to-all | bytes 9437184 | tf_op jit(solution)/shard_map/all_to_all | solution.py:61
  166.9 5.3 %all-to-all-start.1 = ((bf16[16,72,2048]{2,1,0:T(8,128)(2,1)}), bf16[16,72,2048]{2,1,0:T(8,128)(2,1)}, u32[]{:S(2)}, u32[]{:S(2)}) async-start(bf16[16,72,2048]{2,1,0:T(8,128)(2,1)} %bitcast.48), calls=%async_computation.1 | async-start | bytes 9437184 | tf_op jit(solution)/shard_map/all_to_all | solution.py:73
  172.2 12.4 %convolution_convert_fusion.1 = bf16[1152,1536]{1,0:T(8,128)(2,1)} fusion(bf16[1152,2048]{1,0:T(8,128)(2,1)} %bitcast.50, bf16[2048,768]{1,0:T(8,128)(2,1)} %bitcast.58, bf16[2048,768]{1,0:T(8,128)(2,1)} %bitcast.60), kind=kOutput, calls=%fused_computation.8 | convolution fusion | flops 7262109696 | bytes 14548992 | tf_op jit(solution)/shard_map/dot_general | solution.py:67
  184.9 91.3 %all-to-all-done.1 = bf16[16,72,2048]{2,1,0:T(8,128)(2,1)} async-done(((bf16[16,72,2048]{2,1,0:T(8,128)(2,1)}), bf16[16,72,2048]{2,1,0:T(8,128)(2,1)}, u32[]{:S(2)}, u32[]{:S(2)}) %all-to-all-start.1) | async-done | bytes 4718624 | tf_op jit(solution)/shard_map/all_to_all | solution.py:73
  276.1 7.4 %convolution_convert_fusion.3 = bf16[1152,768]{1,0:T(8,128)(2,1)} fusion(bf16[1152,2048]{1,0:T(8,128)(2,1)} %bitcast.5, bf16[1,768,2048]{2,1,0:T(8,128)(2,1)S(1)} %copy-done), kind=kOutput, calls=%fused_computation.25 | convolution fusion | flops 3624763392 | bytes 9633792 | tf_op jit(solution)/shard_map/dot_general | solution.py:85
  284.3 4.5 all-to-all-start
  288.8 3.8 all-to-all-done
  292.8 18.2 %reduce-scatter.2.cloned.1.call-done = bf16[576,768]{1,0:T(8,128)(2,1)} async-done(((bf16[1152,768]{1,0:T(8,128)(2,1)}), bf16[576,768]{1,0:T(8,128)(2,1)}) %reduce-scatter.2.cloned.1.call-update) | async-done | bytes 884752 | tf_op jit(solution)/shard_map/reduce_scatter | solution.py:84
  321.5 7.7 %all-to-all-start.4 = ((bf16[16,1,72]{2,1,0:T(2,128)(2,1)}), bf16[16,1,72]{2,1,0:T(2,128)(2,1)S(1)}, u32[]{:S(2)}, u32[]{:S(2)}) async-start(bf16[16,1,72]{2,1,0:T(2,128)(2,1)} %all_to_all.29), calls=%async_computation.5 | async-start | bytes 16384 | tf_op jit(solution)/shard_map/all_to_all | solution.py:119
  329.2 35.9 %all-gather.2.cloned.1.call-done = bf16[1152,1536]{1,0:T(8,128)(2,1)} async-done(((bf16[576,1536]{1,0:T(8,128)(2,1)}), bf16[1152,1536]{1,0:T(8,128)(2,1)}) %all-gather.2.cloned.1.call-update) | async-done | bytes 3538960 | tf_op jit(solution)/shard_map/all_gather | solution.py:97
  365.1 12.2 %convolution_convert_fusion.2 = bf16[1152,2048]{1,0:T(8,128)(2,1)} fusion(bf16[1152,1536]{1,0:T(8,128)(2,1)} %all-gather.2.cloned.1.call-done, bf16[2048,768]{1,0:T(8,128)(2,1)} %bitcast.59, bf16[2048,768]{1,0:T(8,128)(2,1)} %bitcast.61), kind=kOutput, calls=%fused_computation.9 | convolution fusion | flops 7262699520 | bytes 14548992 | tf_op jit(solution)/shard_map/dot_general | solution.py:108
  377.3 6.5 %all-to-all-start.3 = ((bf16[16,72,2048]{2,1,0:T(8,128)(2,1)}), bf16[16,72,2048]{2,1,0:T(8,128)(2,1)}, u32[]{:S(2)}, u32[]{:S(2)}) async-start(bf16[16,72,2048]{2,1,0:T(8,128)(2,1)} %bitcast.52), calls=%async_computation.4 | async-start | bytes 9437184 | tf_op jit(solution)/shard_map/all_to_all | solution.py:112
  383.9 10.2 %fusion.10 = bf16[1,768,2048]{2,1,0:T(8,128)(2,1)} fusion(bf16[1152,2048]{1,0:T(8,128)(2,1)} %bitcast.5, f32[1152]{0:T(1024)S(1)} %convert_element_type.91, bf16[1152,1536]{1,0:T(8,128)(2,1)} %all-reduce.3.cloned.1.call-done), kind=kOutput, calls=%fused_computation.29 | convolution fusion | flops 3639607296 | bytes 11407872 | tf_op jit(solution)/shard_map/dot_general | solution.py:100
  394.2 6.8 %gather_fusion.2 = bf16[1024]{0:T(1024)(128)(2,1)S(1)} fusion(bf16[1152]{0:T(1024)(128)(2,1)S(1)} %reshape.140, s32[1024]{0:T(1024)S(1)} %broadcast_clamp_fusion), kind=kCustom, calls=%fused_computation.4 | custom fusion | bytes 8192 | tf_op jit(solution)/shard_map/jit(_take)/gather | solution.py:127
  401.8 11.3 %convolution_convert_fusion = bf16[2048,1536]{1,0:T(8,128)(2,1)S(1)} fusion(bf16[1152,2048]{1,0:T(8,128)(2,1)} %bitcast.51, bf16[1152,1536]{1,0:T(8,128)(2,1)} %all-gather.2.cloned.1.call-done), kind=kOutput, calls=%fused_computation.7 | convolution fusion | flops 7250903040 | bytes 14548992 | tf_op jit(solution)/shard_map/dot_general | solution.py:103
  416.3 71.2 %all-to-all-done.3 = bf16[16,72,2048]{2,1,0:T(8,128)(2,1)} async-done(((bf16[16,72,2048]{2,1,0:T(8,128)(2,1)}), bf16[16,72,2048]{2,1,0:T(8,128)(2,1)}, u32[]{:S(2)}, u32[]{:S(2)}) %all-to-all-start.3) | async-done | bytes 4718624 | tf_op jit(solution)/shard_map/all_to_all | solution.py:112
  487.5 11.9 %gather_fusion.1 = bf16[1024,2048]{1,0:T(8,128)(2,1)} fusion(bf16[1152,2048]{1,0:T(8,128)(2,1)} %bitcast.12, s32[1024]{0:T(1024)S(1)} %broadcast_clamp_fusion), kind=kCustom, calls=%fused_computation.3 | custom fusion | bytes 8392704 | tf_op jit(solution)/shard_map/jit(_take)/gather | solution.py:123
  499.4 5.1 %fusion.2 = bf16[128,2048]{1,0:T(8,128)(2,1)} fusion(bf16[1024,2048]{1,0:T(8,128)(2,1)} %gather_fusion.1, pred[128,8]{1,0:T(8,128)(4,1)S(1)} %get-tuple-element.17), kind=kLoop, calls=%fused_computation.18 | loop fusion | flops 3932160 | bytes 4719616 | tf_op jit(solution)/shard_map/reduce_sum | solution.py:124
  (56 shorter events, 17.8 us)
Async XLA Ops:
  7.2 269.0 %copy-start = (bf16[1,768,2048]{2,1,0:T(8,128)(2,1)S(1)}, bf16[1,768,2048]{2,1,0:T(8,128)(2,1)}, u32[]{:S(2)}) copy-start(bf16[1,768,2048]{2,1,0:T(8,128)(2,1)} %param.15) | copy-start | bytes 9437188
  166.9 109.3 %all-to-all-start.1 = ((bf16[16,72,2048]{2,1,0:T(8,128)(2,1)}), bf16[16,72,2048]{2,1,0:T(8,128)(2,1)}, u32[]{:S(2)}, u32[]{:S(2)}) async-start(bf16[16,72,2048]{2,1,0:T(8,128)(2,1)} %bitcast.48), calls=%async_computation.1 | async-start | bytes 9437184 | tf_op jit(solution)/shard_map/all_to_all | solution.py:73
  172.1 120.7 %all-reduce.3.cloned.1.call-start = ((), (), s32[]{:S(2)}) async-start(), calls=%async_computation.7 | async-start | bytes 7077888 | tf_op jit(solution)/shard_map/psum | solution.py:66
  184.6 126.4 %reduce-scatter.2.cloned.1.call-start = ((), (), s32[]{:S(2)}) async-start(), calls=%async_computation.6 | async-start | bytes 2654208 | tf_op jit(solution)/shard_map/reduce_scatter | solution.py:84
  284.3 8.3 %all-to-all-start = ((bf16[16,1,72]{2,1,0:T(2,128)(2,1)}), bf16[16,1,72]{2,1,0:T(2,128)(2,1)S(1)}, u32[]{:S(2)}, u32[]{:S(2)}) async-start(bf16[16,1,72]{2,1,0:T(2,128)(2,1)} %all_to_all.28), calls=%async_computation | async-start | bytes 16384 | tf_op jit(solution)/shard_map/all_to_all | solution.py:74
  288.8 76.3 %all-gather.2.cloned.1.call-start = ((), (), s32[]{:S(2)}) async-start(), calls=%async_computation.8 | async-start | bytes 5308416 | tf_op jit(solution)/shard_map/all_gather | solution.py:97
  314.2 1.4 copy-start.2
  321.5 55.7 %all-to-all-start.4 = ((bf16[16,1,72]{2,1,0:T(2,128)(2,1)}), bf16[16,1,72]{2,1,0:T(2,128)(2,1)S(1)}, u32[]{:S(2)}, u32[]{:S(2)}) async-start(bf16[16,1,72]{2,1,0:T(2,128)(2,1)} %all_to_all.29), calls=%async_computation.5 | async-start | bytes 16384 | tf_op jit(solution)/shard_map/all_to_all | solution.py:119
  377.3 110.2 %all-to-all-start.3 = ((bf16[16,72,2048]{2,1,0:T(8,128)(2,1)}), bf16[16,72,2048]{2,1,0:T(8,128)(2,1)}, u32[]{:S(2)}, u32[]{:S(2)}) async-start(bf16[16,72,2048]{2,1,0:T(8,128)(2,1)} %bitcast.52), calls=%async_computation.4 | async-start | bytes 9437184 | tf_op jit(solution)/shard_map/all_to_all | solution.py:112
  487.5 17.1 %copy-start.1 = (bf16[1,768,2048]{2,1,0:T(8,128)(2,1)S(1)}, bf16[1,768,2048]{2,1,0:T(8,128)(2,1)}, u32[]{:S(2)}) copy-start(bf16[1,768,2048]{2,1,0:T(8,128)(2,1)} %param.15) | copy-start | bytes 9437188
Sparse Core Ops, SparseCore 0:
  184.8 94.8 all-reduce.2
  283.7 27.2 reduce-scatter.1
  315.7 49.3 all-gather.1
where the time goes:
time: 512 us; the launch traced here: 511 us
  waiting for transfers between devices  220 us (43%)
  blocking collectives  114 us (22%)
  local copies, waits for them, and re-layouts  62.6 us (12%)
  matrix products  53.6 us (10%)
  starting transfers between devices  24.2 us (5%)
  other arithmetic  22.1 us (4%)
  between operations  14.6 us (3%)
    all_to_all x1, blocking collectives, per_device(): lax.all_to_all(token_send, 'ep', split_axis=0, concat_axis=0, tiled=True)  110 us
    all_to_all x1, waiting for transfers between devices, per_device(): lax.all_to_all(grad_send, 'ep', split_axis=0, concat_axis=0, tiled=True)  91.3 us
    all_to_all x1, waiting for transfers between devices, per_device(): lax.all_to_all(grad_part.reshape(experts, capacity, width_dev), 'ep', spl...  71.2 us
    all_gather x1, waiting for transfers between devices, per_device(): lax.all_gather(share_grads, 'fs', axis=0, tiled=True)  35.9 us
    reduce_scatter x1, waiting for transfers between devices, per_device(): lax.psum_scatter(lax.dot_general(section, down_local, across_last, prefer...  18.2 us
    dot_general x1, matrix products, per_device(): jnp.dot(section, stacked, preferred_element_type=jnp.float32)  12.4 us
    dot_general x1, matrix products, per_device(): lax.dot_general(grad_gate_up, stacked, across_last, preferred_element_typ...  12.2 us
    gather x1, local copies, waits for them, and re-layouts, per_device(): jnp.take(part_back.reshape(slot_count, width_dev), slot_of, axis=0)  11.9 us
  transfers between devices with their start and end apart: 7, of which 5 were waited for; matrix products, arithmetic and copies ran while one was open for 13% of the time, Pallas kernels for 0%

commit v1 on v0

--- a/solution.py
+++ b/solution.py
@@ -36,13 +36,139 @@
     return (grad_gate_up, grad_prob)
 
 
+def swap(x):
+    return lax.ppermute(x, "fs", [(0, 1), (1, 0)])
+
+
+def in_order(mine, theirs, first):
+    return jnp.concatenate(
+        [jnp.where(first, mine, theirs), jnp.where(first, theirs, mine)], axis=0
+    )
+
+
+def per_device_dense(tokens, cotangent, gate_probs, expert_ids, w_gate, w_up, w_down):
+    tok_dev, top_count = expert_ids.shape
+    experts = lax.axis_size("ep")
+    width_dev = tokens.shape[1]
+    hidden_units = w_gate.shape[2]
+    capacity = slot_capacity(tok_dev, top_count, experts)
+    slot_count = experts * capacity
+    share_rows = slot_count // 2
+    expert = lax.axis_index("ep")
+    share = lax.axis_index("fs")
+    first = share == 0
+    bf16, f32 = jnp.bfloat16, jnp.float32
+
+    packed = jnp.concatenate([expert_ids.astype(bf16), gate_probs], axis=1)
+    packed_all = lax.all_gather(packed, "ep", axis=0)
+    tokens_all = lax.all_gather(tokens, "ep", axis=0)
+    cot_all = lax.all_gather(cotangent, "ep", axis=0)
+
+    named = packed_all[:, :, :top_count] == expert.astype(bf16)
+    chosen = jnp.any(named, axis=2)
+    prob_tok = jnp.sum(
+        jnp.where(named, packed_all[:, :, top_count:], jnp.zeros((), bf16)).astype(f32), axis=2
+    )
+    before = jnp.triu(jnp.ones((tok_dev, tok_dev), bf16), 1)
+    position = jnp.dot(chosen.astype(bf16), before, preferred_element_type=f32).astype(jnp.int32)
+    slot = jnp.where(chosen, position, -1)
+    pick = slot[:, None, :] == jnp.arange(capacity, dtype=jnp.int32)[None, :, None]
+    prob_rows = jnp.sum(jnp.where(pick, prob_tok[:, None, :], 0.0), axis=2).reshape(slot_count)
+    pick = pick.astype(bf16)
+
+    def dispatch(x):
+        return (
+            jnp.einsum("sct,std->scd", pick, x, preferred_element_type=f32)
+            .astype(bf16)
+            .reshape(slot_count, width_dev)
+        )
+
+    across_last = (((1,), (1,)), ((), ()))
+    across_first = (((0,), (0,)), ((), ()))
+    stacked = jnp.concatenate([w_gate[0], w_up[0]], axis=1)
+    down_local = w_down[0]
+
+    def rows_of(x, which):
+        return lax.dynamic_slice_in_dim(x, which * share_rows, share_rows, 0)
+
+    token_rows = dispatch(tokens_all)
+    part_gate_up = jnp.dot(token_rows, stacked, preferred_element_type=f32).astype(bf16)
+    gate_up = (
+        swap(rows_of(part_gate_up, 1 - share)).astype(f32)
+        + rows_of(part_gate_up, share).astype(f32)
+    ).astype(bf16)
+    gate_proj, up_proj, sigmoid_gate, gate_act = activate(gate_up, hidden_units)
+    hidden_mine = (gate_act * up_proj).astype(bf16)
+    hidden = in_order(hidden_mine, swap(hidden_mine), first)
+
+    grad_rows = dispatch(cot_all)
+    part_raw = lax.dot_general(
+        grad_rows, down_local, across_last, preferred_element_type=f32
+    ).astype(bf16)
+    raw = swap(rows_of(part_raw, 1 - share)).astype(f32) + rows_of(part_raw, share).astype(f32)
+    grads_mine, grad_prob_mine = local_grads(
+        raw, gate_up, rows_of(prob_rows, share), hidden_units
+    )
+    grad_gate_up = in_order(grads_mine, swap(grads_mine), first)
+    grad_prob = in_order(grad_prob_mine, swap(grad_prob_mine), first)
+
+    grad_part = lax.dot_general(
+        grad_gate_up, stacked, across_last, preferred_element_type=f32
+    ).astype(bf16)
+    dense = (
+        jnp.einsum(
+            "sct,scd->std",
+            pick,
+            grad_part.reshape(experts, capacity, width_dev),
+            preferred_element_type=f32,
+        )
+        .astype(bf16)
+        .reshape(experts * tok_dev, width_dev)
+    )
+    prob_dense = jnp.sum(
+        pick.astype(f32) * grad_prob.reshape(experts, capacity, 1).astype(f32), axis=1
+    ).astype(bf16)
+    prob_dense = jnp.where(named, prob_dense[:, :, None], jnp.zeros((), bf16)).reshape(
+        experts * tok_dev, top_count
+    )
+    grad_probs = lax.psum_scatter(prob_dense, "ep", scatter_dimension=0, tiled=True)
+    grad_tokens = lax.psum_scatter(dense, "ep", scatter_dimension=0, tiled=True)
+
+    weighted = (prob_rows[:, None] * grad_rows.astype(f32)).astype(bf16)
+    new_down = lax.dot_general(
+        hidden, weighted, across_first, preferred_element_type=f32
+    ).astype(bf16)
+    new_gate = lax.dot_general(
+        token_rows, grad_gate_up[:, :hidden_units], across_first, preferred_element_type=f32
+    ).astype(bf16)
+    new_up = lax.dot_general(
+        token_rows, grad_gate_up[:, hidden_units:], across_first, preferred_element_type=f32
+    ).astype(bf16)
+    return (grad_tokens, grad_probs, new_gate[None], new_up[None], new_down[None])
+
+
+def slot_capacity(tok_dev, top_count, experts):
+    return (9 * tok_dev * top_count + 8 * experts - 1) // (8 * experts)
+
+
 def per_device(tokens, cotangent, gate_probs, expert_ids, w_gate, w_up, w_down):
+    tok_dev, top_count = expert_ids.shape
+    experts = lax.axis_size("ep")
+    dense_rows_fit = tok_dev <= 2 * slot_capacity(tok_dev, top_count, experts)
+    if lax.axis_size("fs") == 2 and experts <= 256 and dense_rows_fit:
+        return per_device_dense(
+            tokens, cotangent, gate_probs, expert_ids, w_gate, w_up, w_down
+        )
+    return per_device_slots(tokens, cotangent, gate_probs, expert_ids, w_gate, w_up, w_down)
+
+
+def per_device_slots(tokens, cotangent, gate_probs, expert_ids, w_gate, w_up, w_down):
     tok_dev, top_count = expert_ids.shape
     experts = lax.axis_size("ep")
     shards = lax.axis_size("fs")
     width_dev = tokens.shape[1]
     hidden_units = w_gate.shape[2]
-    capacity = (9 * tok_dev * top_count + 8 * experts - 1) // (8 * experts)
+    capacity = slot_capacity(tok_dev, top_count, experts)
     slot_count = experts * capacity
     share_rows = slot_count // shards
     slot_of, filled_by = build_slots(expert_ids, experts, capacity)

time: 512 us -> 375 us (0.73)
  blocking collectives: 114 us -> 16.1 us
  local copies, waits for them, and re-layouts: 62.6 us -> 8.97 us
  waiting for transfers between devices: 220 us -> 257 us
  starting transfers between devices: 24.2 us -> 6.3 us
  other arithmetic: 22.1 us -> 12.8 us
    all_to_all x4 -> x0, waiting for transfers between devices: 166 us -> none  [the longest x1 91.3 us: per_device(): lax.all_to_all(grad_send, 'ep', split_axis=0, concat_axis=0, tiled=True)]
    all_to_all x1 -> x0, blocking collectives: 110 us -> none  [per_device(): lax.all_to_all(token_send, 'ep', split_axis=0, concat_axis=0, tiled=True)]
    all_gather x1 -> x2, waiting for transfers between devices: 35.9 us -> 117 us  [the longest x1 58.5 us: per_device_dense(): tokens_all = lax.all_gather(tokens, 'ep', axis=0)]
    ppermute x0 -> x5, waiting for transfers between devices: none -> 69.3 us  [swap(): return lax.ppermute(x, 'fs', [(0, 1), (1, 0)])]
    reduce_scatter x1, waiting for transfers between devices: 18.2 us -> 68.8 us  [per_device_dense(): grad_tokens = lax.psum_scatter(dense, 'ep', scatter_dimension=0, tiled=True)]
    gather x6 -> x0, local copies, waits for them, and re-layouts: 49.6 us -> none  [the longest x1 11.9 us: per_device(): jnp.take(part_back.reshape(slot_count, width_dev), slot_of, axis=0)]
    all_to_all x4 -> x0, starting transfers between devices: 23.9 us -> none  [the longest x1 7.66 us: per_device(): lax.all_to_all(grad_prob.reshape(experts, capacity), 'ep', split_axis=0,...]
    all_gather x0 -> x1, blocking collectives: none -> 16.1 us  [per_device_dense(): packed_all = lax.all_gather(packed, 'ep', axis=0)]
  transfers between devices with their start and end apart: 7 -> 9, of which waited for: 5 -> 8; matrix products, arithmetic and copies ran while one was open for 13% -> 19% of each run, Pallas kernels for 0% -> 0%
where the time goes in v1:
time: 375 us; the launch traced here: 373 us
  waiting for transfers between devices  257 us (69%)
  matrix products  57.5 us (15%)
  blocking collectives  16.1 us (4%)
  between operations  14.1 us (4%)
  other arithmetic  12.8 us (3%)
  local copies, waits for them, and re-layouts  8.97 us (2%)
  starting transfers between devices  6.3 us (2%)
    ppermute x5, waiting for transfers between devices, swap(): return lax.ppermute(x, 'fs', [(0, 1), (1, 0)])  69.3 us
    reduce_scatter x1, waiting for transfers between devices, per_device_dense(): grad_tokens = lax.psum_scatter(dense, 'ep', scatter_dimension=0, tiled=True)  68.8 us
    all_gather x1, waiting for transfers between devices, per_device_dense(): tokens_all = lax.all_gather(tokens, 'ep', axis=0)  58.5 us
    all_gather x1, waiting for transfers between devices, per_device_dense(): cot_all = lax.all_gather(cotangent, 'ep', axis=0)  58.4 us
    all_gather x1, blocking collectives, per_device_dense(): packed_all = lax.all_gather(packed, 'ep', axis=0)  16.1 us
    dot_general x2, matrix products, dispatch(): jnp.einsum('sct,std->scd', pick, x, preferred_element_type=f32).astype(bf16)  9.67 us
    dot_general x1, matrix products, per_device_dense(): lax.dot_general(hidden, weighted, across_first, preferred_element_type=f32)  9.36 us
    dot_general x1, matrix products, per_device_dense(): jnp.dot(token_rows, stacked, preferred_element_type=f32).astype(bf16)  7.89 us
  transfers between devices with their start and end apart: 9, of which 8 were waited for; matrix products, arithmetic and copies ran while one was open for 19% of the time, Pallas kernels for 0%

profile of v1, /device:TPU:11, one launch (start us, length us, event | category | flops | bytes accessed | tf_op | source)
XLA Modules:
  0.0 372.8 jit_solution(17014572784711877965)
XLA Ops:
  10.1 16.1 %all-gather = bf16[2048,16]{0,1:T(8,128)(2,1)S(1)} all-gather(bf16[128,16]{0,1:T(8,128)(2,1)S(1)} %pad_maximum_fusion.6), channel_id=2, replica_groups=mesh['ep'=16,'fs'=2] {'ep'}, dimensions={0}, use_global_device_ids=true | all-gather | bytes 69632 | tf_op jit(solution)/shard_map/all_gather | solution.py:63
  26.5 58.5 %all-gather.8.cloned.1.call-done = bf16[2048,2048]{1,0:T(8,128)(2,1)} async-done(((bf16[128,2048]{1,0:T(8,128)(2,1)}), bf16[2048,2048]{1,0:T(8,128)(2,1)}) %all-gather.8.cloned.1.call-update) | async-done | bytes 8388624 | tf_op jit(solution)/shard_map/all_gather | solution.py:64
  85.0 4.9 %convolution_convert_fusion.3 = bf16[16,72,2048]{2,1,0:T(8,128)(2,1)S(1)} fusion(bf16[16,128,2048]{2,1,0:T(8,128)(2,1)} %bitcast.34, s32[16,128]{1,0:T(8,128)S(1)} %fusion.23), kind=kOutput, calls=%fused_computation.12 | convolution fusion | flops 606486528 | bytes 13115392 | tf_op jit(solution)/shard_map/sct,std->scd/dot_general | solution.py:81
  90.2 7.9 %convolution_convert_fusion = bf16[1152,1536]{1,0:T(8,128)(2,1)S(1)} fusion(bf16[1152,2048]{1,0:T(8,128)(2,1)S(1)} %bitcast.35, bf16[2048,768]{1,0:T(8,128)(2,1)S(1)} %bitcast.45, bf16[2048,768]{1,0:T(8,128)(2,1)S(1)} %bitcast.47), kind=kOutput, calls=%fused_computation.1 | convolution fusion | flops 7262109696 | bytes 14548992 | tf_op jit(solution)/shard_map/dot_general | solution.py:95
  98.2 1.4 constant_dynamic-slice_fusion
  101.6 58.4 %all-gather.6.cloned.1.call-done = bf16[2048,2048]{1,0:T(8,128)(2,1)} async-done(((bf16[128,2048]{1,0:T(8,128)(2,1)}), bf16[2048,2048]{1,0:T(8,128)(2,1)}) %all-gather.6.cloned.1.call-update) | async-done | bytes 8388624 | tf_op jit(solution)/shard_map/all_gather | solution.py:65
  160.1 4.8 %convolution_convert_fusion.4 = bf16[16,72,2048]{2,1,0:T(8,128)(2,1)S(1)} fusion(bf16[16,128,2048]{2,1,0:T(8,128)(2,1)} %bitcast.33, s32[16,128]{1,0:T(8,128)S(1)} %fusion.23), kind=kOutput, calls=%fused_computation.13 | convolution fusion | flops 606486528 | bytes 13115392 | tf_op jit(solution)/shard_map/sct,std->scd/dot_general | solution.py:81
  164.9 3.9 %convolution_convert_fusion.7 = bf16[1152,768]{1,0:T(8,128)(2,1)S(1)} fusion(bf16[1152,2048]{1,0:T(8,128)(2,1)S(1)} %bitcast.40, bf16[1,768,2048]{2,1,0:T(8,128)(2,1)S(1)} %copy-done), kind=kOutput, calls=%fused_computation.18 | convolution fusion | flops 3624763392 | bytes 9633792 | tf_op jit(solution)/shard_map/dot_general | solution.py:105
  171.5 2.6 add_convert_fusion
  174.0 17.4 %collective-permute-done = bf16[576,768]{1,0:T(8,128)(2,1)S(1)} collective-permute-done((bf16[576,768]{1,0:T(8,128)(2,1)}, bf16[576,768]{1,0:T(8,128)(2,1)S(1)}, u32[]{:S(2)}, u32[]{:S(2)}) %collective-permute-start) | collective-permute-done | bytes 884768 | tf_op jit(solution)/shard_map/ppermute | solution.py:40
  191.4 1.7 multiply_reduce_fusion
  194.3 1.3 collective-permute-done.3
  196.5 2.5 fusion.9
  202.6 35.5 %collective-permute-done.2 = bf16[576,1536]{1,0:T(8,128)(2,1)} collective-permute-done((bf16[576,1536]{1,0:T(8,128)(2,1)S(1)}, bf16[576,1536]{1,0:T(8,128)(2,1)}, u32[]{:S(2)}, u32[]{:S(2)}) %collective-permute-start.2) | collective-permute-done | bytes 1769504 | tf_op jit(solution)/shard_map/ppermute | solution.py:40
  238.2 2.4 broadcast_select_fusion.1
  240.6 7.8 %convolution_convert_fusion.1 = bf16[1152,2048]{1,0:T(8,128)(2,1)S(1)} fusion(bf16[2048,768]{1,0:T(8,128)(2,1)S(1)} %bitcast.46, bf16[2048,768]{1,0:T(8,128)(2,1)S(1)} %bitcast.48, bf16[576,1536]{1,0:T(8,128)(2,1)S(1)} %get-tuple-element.14, bf16[576,1536]{1,0:T(8,128)(2,1)S(1)} %get-tuple-element.13), kind=kOutput, calls=%fused_computation.2 | convolution fusion | flops 7269777408 | bytes 14548992 | tf_op jit(solution)/shard_map/dot_general | solution.py:115
  248.4 5.8 %convolution_convert_fusion.2 = bf16[16,128,2048]{2,1,0:T(8,128)(2,1)} fusion(bf16[16,72,2048]{2,1,0:T(8,128)(2,1)S(1)} %bitcast.42, s32[16,128]{1,0:T(8,128)S(1)} %fusion.23), kind=kOutput, calls=%fused_computation.4 | convolution fusion | flops 608321536 | bytes 13115392 | tf_op jit(solution)/shard_map/sct,scd->std/dot_general | solution.py:119
  257.0 1.4 copy.17
  258.4 15.1 %collective-permute-done.4 = bf16[576,768]{1,0:T(8,128)(2,1)} collective-permute-done((bf16[576,768]{1,0:T(8,128)(2,1)S(1)}, bf16[576,768]{1,0:T(8,128)(2,1)}, u32[]{:S(2)}, u32[]{:S(2)}) %collective-permute-start.4) | collective-permute-done | bytes 884768 | tf_op jit(solution)/shard_map/ppermute | solution.py:40
  273.5 1.5 broadcast_select_fusion.3
  275.1 9.4 %fusion.6 = bf16[1,768,2048]{2,1,0:T(8,128)(2,1)} fusion(bf16[1152,2048]{1,0:T(8,128)(2,1)} %bitcast.41, f32[1152]{0:T(1024)S(1)} %reshape.57, bf16[576,768]{1,0:T(8,128)(2,1)S(1)} %get-tuple-element.16, bf16[576,768]{1,0:T(8,128)(2,1)S(1)} %get-tuple-element.15), kind=kOutput, calls=%fused_computation.22 | convolution fusion | flops 3636068352 | bytes 9638400 | tf_op jit(solution)/shard_map/dot_general | solution.py:138
  284.4 5.8 %fusion.4 = bf16[1,2048,768]{2,1,0:T(8,128)(2,1)} fusion(bf16[1152,2048]{1,0:T(8,128)(2,1)S(1)} %bitcast.38, bf16[576,1536]{1,0:T(8,128)(2,1)S(1)} %get-tuple-element.13, bf16[576,1536]{1,0:T(8,128)(2,1)S(1)} %copy-done.12), kind=kOutput, calls=%fused_computation.20 | convolution fusion | flops 3628990464 | bytes 11403264 | tf_op jit(solution)/shard_map/dot_general | solution.py:141
  290.3 7.2 %fusion.5 = bf16[1,2048,768]{2,1,0:T(8,128)(2,1)} fusion(bf16[1152,2048]{1,0:T(8,128)(2,1)S(1)} %bitcast.39, bf16[576,1536]{1,0:T(8,128)(2,1)} %copy-done.10, bf16[576,1536]{1,0:T(8,128)(2,1)S(1)} %copy-done.12), kind=kOutput, calls=%fused_computation.21 | convolution fusion | flops 3628990464 | bytes 11403264 | tf_op jit(solution)/shard_map/dot_general | solution.py:144
  297.4 68.8 %reduce-scatter.5.cloned.1.call-done = bf16[128,2048]{1,0:T(8,128)(2,1)} async-done(((bf16[2048,2048]{1,0:T(8,128)(2,1)}), bf16[128,2048]{1,0:T(8,128)(2,1)}) %reduce-scatter.5.cloned.1.call-update) | async-done | bytes 524304 | tf_op jit(solution)/shard_map/reduce_scatter | solution.py:135
  (72 shorter events, 16.7 us)
Async XLA Ops:
  7.2 157.7 %copy-start = (bf16[1,768,2048]{2,1,0:T(8,128)(2,1)S(1)}, bf16[1,768,2048]{2,1,0:T(8,128)(2,1)}, u32[]{:S(2)}) copy-start(bf16[1,768,2048]{2,1,0:T(8,128)(2,1)} %param.13) | copy-start | bytes 9437188
  7.2 77.8 %all-gather.8.cloned.1.call-start = ((), (), s32[]{:S(2)}) async-start(), calls=%async_computation.4 | async-start | bytes 8912896 | tf_op jit(solution)/shard_map/all_gather | solution.py:64
  7.9 152.2 %all-gather.6.cloned.1.call-start = ((), (), s32[]{:S(2)}) async-start(), calls=%async_computation.3 | async-start | bytes 8912896 | tf_op jit(solution)/shard_map/all_gather | solution.py:65
  8.7 248.4 %reduce-scatter.7.cloned.1.call-start = ((), (), s32[]{:S(2)}) async-start(), calls=%async_computation.5 | async-start | bytes 557056
  85.0 4.9 %copy-start.13 = (bf16[1,2048,768]{2,1,0:T(8,128)(2,1)S(1)}, bf16[1,2048,768]{2,1,0:T(8,128)(2,1)}, u32[]{:S(2)}) copy-start(bf16[1,2048,768]{2,1,0:T(8,128)(2,1)} %param.12) | copy-start | bytes 9437188
  85.0 5.2 %copy-start.15 = (bf16[1,2048,768]{2,1,0:T(8,128)(2,1)S(1)}, bf16[1,2048,768]{2,1,0:T(8,128)(2,1)}, u32[]{:S(2)}) copy-start(bf16[1,2048,768]{2,1,0:T(8,128)(2,1)} %param.11) | copy-start | bytes 9437188
  89.9 8.2 %copy-start.2 = (bf16[16,72,2048]{2,1,0:T(8,128)(2,1)}, bf16[16,72,2048]{2,1,0:T(8,128)(2,1)S(1)}, u32[]{:S(2)}) copy-start(bf16[16,72,2048]{2,1,0:T(8,128)(2,1)S(1)} %convolution_convert_fusion.3) | copy-start | bytes 14155780
  100.5 71.0 %collective-permute-start.1 = (bf16[576,1536]{1,0:T(8,128)(2,1)}, bf16[576,1536]{1,0:T(8,128)(2,1)}, u32[]{:S(2)}, u32[]{:S(2)}) collective-permute-start(bf16[576,1536]{1,0:T(8,128)(2,1)} %constant_dynamic-slice_fusion), channel_id=1, source_target_pairs={{0,1},{1,0},{2,3},{3,2},{4,5},{5,4},{6,7},{7,6},{8,9},{9,8},{10,11... | collective-permute-start | bytes 5308424 | tf_op jit(solution)/shard_map/ppermute | solution.py:40
  164.8 3.9 %copy-start.3 = (bf16[16,72,2048]{2,1,0:T(8,128)(2,1)}, bf16[16,72,2048]{2,1,0:T(8,128)(2,1)S(1)}, u32[]{:S(2)}) copy-start(bf16[16,72,2048]{2,1,0:T(8,128)(2,1)S(1)} %convolution_convert_fusion.4) | copy-start | bytes 14155780
  170.3 21.2 %collective-permute-start = (bf16[576,768]{1,0:T(8,128)(2,1)}, bf16[576,768]{1,0:T(8,128)(2,1)S(1)}, u32[]{:S(2)}, u32[]{:S(2)}) collective-permute-start(bf16[576,768]{1,0:T(8,128)(2,1)} %constant_dynamic-slice_fusion.1), channel_id=1, source_target_pairs={{0,1},{1,0},{2,3},{3,2},{4,5},{5,4},{6,7},{7,6},{8,9},{9,8},{10,11... | collective-permute-start | bytes 2654216 | tf_op jit(solution)/shard_map/ppermute | solution.py:40
  171.5 20.0 %copy-start.6 = (bf16[1152,768]{1,0:T(8,128)(2,1)S(1)}, bf16[1152,768]{1,0:T(8,128)(2,1)}, u32[]{:S(2)}) copy-start(bf16[1152,768]{1,0:T(8,128)(2,1)} %copy-done.5) | copy-start | bytes 5308420
  191.4 5.0 %copy-start.8 = (bf16[576,768]{1,0:T(8,128)(2,1)}, bf16[576,768]{1,0:T(8,128)(2,1)S(1)}, u32[]{:S(2)}) copy-start(bf16[576,768]{1,0:T(8,128)(2,1)S(1)} %collective-permute-done) | copy-start | bytes 2654212
  193.1 2.4 collective-permute-start.3
  200.1 38.1 %collective-permute-start.2 = (bf16[576,1536]{1,0:T(8,128)(2,1)S(1)}, bf16[576,1536]{1,0:T(8,128)(2,1)}, u32[]{:S(2)}, u32[]{:S(2)}) collective-permute-start(bf16[576,1536]{1,0:T(8,128)(2,1)S(1)} %pad_maximum_fusion.5), channel_id=1, source_target_pairs={{0,1},{1,0},{2,3},{3,2},{4,5},{5,4},{6,7},{7,6},{8,9},{9,8},{10,11... | collective-permute-start | bytes 5308424 | tf_op jit(solution)/shard_map/ppermute | solution.py:40
  202.4 163.9 %reduce-scatter.5.cloned.1.call-start = ((), (), s32[]{:S(2)}) async-start(), calls=%async_computation.2 | async-start | bytes 8912896 | tf_op jit(solution)/shard_map/reduce_scatter | solution.py:135
  202.6 38.0 %copy-start.14 = (bf16[1,2048,768]{2,1,0:T(8,128)(2,1)S(1)}, bf16[1,2048,768]{2,1,0:T(8,128)(2,1)}, u32[]{:S(2)}) copy-start(bf16[1,2048,768]{2,1,0:T(8,128)(2,1)} %param.12) | copy-start | bytes 9437188
  202.6 37.9 %copy-start.16 = (bf16[1,2048,768]{2,1,0:T(8,128)(2,1)S(1)}, bf16[1,2048,768]{2,1,0:T(8,128)(2,1)}, u32[]{:S(2)}) copy-start(bf16[1,2048,768]{2,1,0:T(8,128)(2,1)} %param.11) | copy-start | bytes 9437188
  240.5 7.9 %copy-start.11 = (bf16[576,1536]{1,0:T(8,128)(2,1)}, bf16[576,1536]{1,0:T(8,128)(2,1)S(1)}, u32[]{:S(2)}) copy-start(bf16[576,1536]{1,0:T(8,128)(2,1)S(1)} %get-tuple-element.14) | copy-start | bytes 5308420
  240.5 43.9 %copy-start.10 = (bf16[576,1536]{1,0:T(8,128)(2,1)}, bf16[576,1536]{1,0:T(8,128)(2,1)S(1)}, u32[]{:S(2)}) copy-start(bf16[576,1536]{1,0:T(8,128)(2,1)S(1)} %get-tuple-element.13) | copy-start | bytes 5308420
  255.3 18.2 %collective-permute-start.4 = (bf16[576,768]{1,0:T(8,128)(2,1)S(1)}, bf16[576,768]{1,0:T(8,128)(2,1)}, u32[]{:S(2)}, u32[]{:S(2)}) collective-permute-start(bf16[576,768]{1,0:T(8,128)(2,1)S(1)} %copy-done.9), channel_id=1, source_target_pairs={{0,1},{1,0},{2,3},{3,2},{4,5},{5,4},{6,7},{7,6},{8,9},{9,8},{10,11... | collective-permute-start | bytes 2654216 | tf_op jit(solution)/shard_map/ppermute | solution.py:40
  273.5 10.9 %slice-start = ((s8[4718592]{0:T(1024)(128)(4,1)}), s8[4194304]{0:T(1024)(128)(4,1)S(1)}, s32[]{:S(2)}) async-start(s8[4718592]{0:T(1024)(128)(4,1)} %bitcast.36), calls=%async_computation.6 | async-start | bytes 8388608
  275.0 9.4 %slice-start.1 = ((s8[4718592]{0:T(1024)(128)(4,1)}), s8[524288]{0:T(1024)(128)(4,1)S(1)}, s32[]{:S(2)}) async-start(s8[4718592]{0:T(1024)(128)(4,1)} %bitcast.36), calls=%async_computation.7 | async-start | bytes 1048576
  275.0 9.4 %copy-start.12 = (bf16[576,1536]{1,0:T(8,128)(2,1)S(1)}, bf16[576,1536]{1,0:T(8,128)(2,1)}, u32[]{:S(2)}) copy-start(bf16[576,1536]{1,0:T(8,128)(2,1)} %copy-done.11) | copy-start | bytes 5308420
  290.3 76.0 %copy-start.1 = (bf16[1,768,2048]{2,1,0:T(8,128)(2,1)S(1)}, bf16[1,768,2048]{2,1,0:T(8,128)(2,1)}, u32[]{:S(2)}) copy-start(bf16[1,768,2048]{2,1,0:T(8,128)(2,1)} %param.13) | copy-start | bytes 9437188
  (4 other events, 5.9 us)
Sparse Core Ops, SparseCore 0:
  10.2 74.7 all-gather.7
  87.2 72.8 all-gather.5
  202.5 54.5 reduce-scatter.6
  261.5 104.6 reduce-scatter.4

commit v2 on v1

--- a/solution.py
+++ b/solution.py
@@ -1,6 +1,8 @@
 import jax
 import jax.numpy as jnp
 from jax import lax
+from jax.experimental import pallas as pl
+from jax.experimental.pallas import tpu as pltpu
 from jax.sharding import PartitionSpec as P
 
 
@@ -34,6 +36,105 @@
     )
     grad_prob = jnp.sum(hidden.astype(jnp.float32) * raw_grad, axis=1).astype(jnp.bfloat16)
     return (grad_gate_up, grad_prob)
+
+
+def far_hops(count):
+    return list(range(4, count, 4))
+
+
+def greet(me, count):
+    barrier = pltpu.get_barrier_semaphore()
+    partners = [1, 2] + far_hops(count)
+    for hop in partners:
+        pl.semaphore_signal(
+            barrier,
+            inc=1,
+            device_id={"ep": lax.bitwise_xor(me, hop)},
+            device_id_type=pl.DeviceIdType.MESH,
+        )
+    pl.semaphore_wait(barrier, len(partners))
+
+
+def gather_kernel(arrays, count, *refs):
+    blocks, outs = refs[:arrays], refs[arrays : 2 * arrays]
+    stages = refs[2 * arrays : 3 * arrays]
+    send_sem, recv_sem, load_sem, store_sem = refs[3 * arrays :]
+    me = lax.axis_index("ep")
+    loads = [
+        pltpu.make_async_copy(blocks[i], stages[i], load_sem.at[i]) for i in range(arrays)
+    ]
+    stores = [
+        pltpu.make_async_copy(stages[i], outs[i].at[0], store_sem.at[i]) for i in range(arrays)
+    ]
+    for load in loads:
+        load.start()
+    greet(me, count)
+
+    def send(i, source, hop):
+        return pltpu.make_async_remote_copy(
+            src_ref=blocks[i] if source == 0 else outs[i].at[source],
+            dst_ref=outs[i].at[source + hop],
+            send_sem=send_sem.at[i, source + hop],
+            recv_sem=recv_sem.at[i, source + hop],
+            device_id={"ep": lax.bitwise_xor(me, hop)},
+            device_id_type=pl.DeviceIdType.MESH,
+        )
+
+    copies = {}
+
+    def start(source, hop):
+        for i in range(arrays):
+            copies[i, source + hop] = send(i, source, hop)
+            copies[i, source + hop].start()
+
+    def arrived(slot):
+        for i in range(arrays):
+            copies[i, slot].wait_recv()
+
+    far = far_hops(count)
+    for hop in far:
+        start(0, hop)
+    start(0, 2)
+    start(0, 1)
+    for load, store in zip(loads, stores):
+        load.wait()
+        store.start()
+    for slot in far:
+        arrived(slot)
+        start(slot, 2)
+        start(slot, 1)
+    for slot in [0] + far:
+        arrived(slot + 2)
+        start(slot + 2, 1)
+    for slot in [0] + far:
+        arrived(slot + 1)
+        arrived(slot + 3)
+    for copy in copies.values():
+        copy.wait_send()
+    for store in stores:
+        store.wait()
+
+
+def gather(collective_id, *blocks):
+    count = lax.axis_size("ep")
+    arrays = len(blocks)
+    return pl.pallas_call(
+        lambda *refs: gather_kernel(arrays, count, *refs),
+        out_shape=[jax.ShapeDtypeStruct((count,) + b.shape, b.dtype) for b in blocks],
+        in_specs=[pl.BlockSpec(memory_space=pl.ANY)] * arrays,
+        out_specs=[pl.BlockSpec(memory_space=pl.ANY)] * arrays,
+        scratch_shapes=[pltpu.VMEM(b.shape, b.dtype) for b in blocks]
+        + [
+            pltpu.SemaphoreType.DMA((arrays, count)),
+            pltpu.SemaphoreType.DMA((arrays, count)),
+            pltpu.SemaphoreType.DMA((arrays,)),
+            pltpu.SemaphoreType.DMA((arrays,)),
+        ],
+        compiler_params=pltpu.CompilerParams(
+            collective_id=collective_id, has_side_effects=True
+        ),
+        name=f"gather_{collective_id}",
+    )(*blocks)
 
 
 def swap(x):
@@ -60,14 +161,13 @@
     bf16, f32 = jnp.bfloat16, jnp.float32
 
     packed = jnp.concatenate([expert_ids.astype(bf16), gate_probs], axis=1)
-    packed_all = lax.all_gather(packed, "ep", axis=0)
-    tokens_all = lax.all_gather(tokens, "ep", axis=0)
-    cot_all = lax.all_gather(cotangent, "ep", axis=0)
+    packed = jnp.pad(packed, ((0, 0), (0, 128 - 2 * top_count)))
+    tokens_all, packed_all = gather(0, tokens, packed)
 
     named = packed_all[:, :, :top_count] == expert.astype(bf16)
     chosen = jnp.any(named, axis=2)
     prob_tok = jnp.sum(
-        jnp.where(named, packed_all[:, :, top_count:], jnp.zeros((), bf16)).astype(f32), axis=2
+        jnp.where(named, packed_all[:, :, top_count : 2 * top_count], jnp.zeros((), bf16)).astype(f32), axis=2
     )
     before = jnp.triu(jnp.ones((tok_dev, tok_dev), bf16), 1)
     position = jnp.dot(chosen.astype(bf16), before, preferred_element_type=f32).astype(jnp.int32)
@@ -93,8 +193,11 @@
 
     token_rows = dispatch(tokens_all)
     part_gate_up = jnp.dot(token_rows, stacked, preferred_element_type=f32).astype(bf16)
+    part_theirs = swap(rows_of(part_gate_up, 1 - share))
+    cotangent, part_gate_up = lax.optimization_barrier((cotangent, part_gate_up))
+    (cot_all,) = gather(1, cotangent)
     gate_up = (
-        swap(rows_of(part_gate_up, 1 - share)).astype(f32)
+        part_theirs.astype(f32)
         + rows_of(part_gate_up, share).astype(f32)
     ).astype(bf16)
     gate_proj, up_proj, sigmoid_gate, gate_act = activate(gate_up, hidden_units)
@@ -131,6 +234,11 @@
     prob_dense = jnp.where(named, prob_dense[:, :, None], jnp.zeros((), bf16)).reshape(
         experts * tok_dev, top_count
     )
+    source = lax.bitwise_xor(jnp.arange(experts, dtype=jnp.int32), expert)
+    prob_dense = jnp.take(prob_dense.reshape(experts, tok_dev, top_count), source, axis=0)
+    prob_dense = prob_dense.reshape(experts * tok_dev, top_count)
+    dense = jnp.take(dense.reshape(experts, tok_dev, width_dev), source, axis=0)
+    dense = dense.reshape(experts * tok_dev, width_dev)
     grad_probs = lax.psum_scatter(prob_dense, "ep", scatter_dimension=0, tiled=True)
     grad_tokens = lax.psum_scatter(dense, "ep", scatter_dimension=0, tiled=True)
 
@@ -155,7 +263,7 @@
     tok_dev, top_count = expert_ids.shape
     experts = lax.axis_size("ep")
     dense_rows_fit = tok_dev <= 2 * slot_capacity(tok_dev, top_count, experts)
-    if lax.axis_size("fs") == 2 and experts <= 256 and dense_rows_fit:
+    if lax.axis_size("fs") == 2 and experts == 16 and dense_rows_fit:
         return per_device_dense(
             tokens, cotangent, gate_probs, expert_ids, w_gate, w_up, w_down
         )

time: 375 us -> 387 us (1.032)
  Pallas kernels: 0 us -> 133 us
  waiting for transfers between devices: 257 us -> 136 us
  blocking collectives: 16.1 us -> 0 us
  local copies, waits for them, and re-layouts: 8.97 us -> 20.7 us
  other arithmetic: 12.8 us -> 22.5 us
  starting transfers between devices: 6.3 us -> 2.23 us
    pallas_call x0 -> x2, Pallas kernels: none -> 133 us  [gather(): pl.pallas_call(lambda *refs: gather_kernel(arrays, count, *refs), out_sha...]
    all_gather x2 -> x0, waiting for transfers between devices: 117 us -> none  [the longest x1 58.5 us: per_device_dense(): tokens_all = lax.all_gather(tokens, 'ep', axis=0)]
    all_gather x1 -> x0, blocking collectives: 16.1 us -> none  [per_device_dense(): packed_all = lax.all_gather(packed, 'ep', axis=0)]
    gather x0 -> x3, local copies, waits for them, and re-layouts: none -> 10.8 us  [the longest x1 8.2 us: per_device_dense(): dense = jnp.take(dense.reshape(experts, tok_dev, width_dev), source, axis=0)]
    select_n x0 -> x4, other arithmetic: none -> 7.82 us  [the longest x2 7.46 us: per_device_dense(): dense = jnp.take(dense.reshape(experts, tok_dev, width_dev), source, axis=0)]
  transfers between devices with their start and end apart: 9 -> 7, of which waited for: 8 -> 5; matrix products, arithmetic and copies ran while one was open for 19% -> 18% of each run, Pallas kernels for 0% -> 17%
where the time goes in v2:
time: 387 us; the launch traced here: 385 us
  waiting for transfers between devices  136 us (35%)
  Pallas kernels  133 us (34%)
  matrix products  56.1 us (14%)
  other arithmetic  22.5 us (6%)
  local copies, waits for them, and re-layouts  20.7 us (5%)
  between operations  14.4 us (4%)
    pallas_call x2, Pallas kernels, gather(): pl.pallas_call(lambda *refs: gather_kernel(arrays, count, *refs), out_sha...  133 us
    ppermute x5, waiting for transfers between devices, swap(): return lax.ppermute(x, 'fs', [(0, 1), (1, 0)])  71.2 us
    reduce_scatter x1, waiting for transfers between devices, per_device_dense(): grad_tokens = lax.psum_scatter(dense, 'ep', scatter_dimension=0, tiled=True)  65 us
    dot_general x2, matrix products, dispatch(): jnp.einsum('sct,std->scd', pick, x, preferred_element_type=f32).astype(bf16)  9.67 us
    dot_general x1, matrix products, per_device_dense(): lax.dot_general(hidden, weighted, across_first, preferred_element_type=f32)  8.97 us
    gather x1, local copies, waits for them, and re-layouts, per_device_dense(): dense = jnp.take(dense.reshape(experts, tok_dev, width_dev), source, axis=0)  8.2 us
    dot_general x1, matrix products, per_device_dense(): jnp.dot(token_rows, stacked, preferred_element_type=f32).astype(bf16)  8.07 us
    dot_general x1, matrix products, per_device_dense(): lax.dot_general(grad_gate_up, stacked, across_last, preferred_element_typ...  8.06 us
  transfers between devices with their start and end apart: 7, of which 5 were waited for; matrix products, arithmetic and copies ran while one was open for 18% of the time, Pallas kernels for 17%

profile of v2, /device:TPU:11, one launch (start us, length us, event | category | flops | bytes accessed | tf_op | source)
XLA Modules:
  0.0 384.7 jit_solution(6309420836824043244)
XLA Ops:
  9.6 67.5 %gather_0.1 = (bf16[16,128,2048]{2,1,0:T(8,128)(2,1)}, bf16[16,128,128]{2,1,0:T(8,128)(2,1)}) custom-call(bf16[128,2048]{1,0:T(8,128)(2,1)} %refs_0_.1, bf16[128,128]{1,0:T(8,128)(2,1)} %pad.4.refs_1_), custom_call_target="tpu_custom_call" | custom-call | tf_op jit(solution)/shard_map/gather_0/pallas_call | solution.py:121
  77.1 1.8 convert_reduce_fusion
  79.3 4.9 %convolution_convert_fusion.4 = bf16[16,72,2048]{2,1,0:T(8,128)(2,1)S(1)} fusion(bf16[16,128,2048]{2,1,0:T(8,128)(2,1)} %get-tuple-element.10, s32[16,128]{1,0:T(8,128)S(1)} %fusion.23), kind=kOutput, calls=%fused_computation.16 | convolution fusion | flops 606486528 | bytes 13115392 | tf_op jit(solution)/shard_map/sct,std->scd/dot_general | solution.py:181
  84.6 8.1 %convolution_convert_fusion = bf16[1152,1536]{1,0:T(8,128)(2,1)S(1)} fusion(bf16[1152,2048]{1,0:T(8,128)(2,1)S(1)} %bitcast.30, bf16[2048,768]{1,0:T(8,128)(2,1)S(1)} %bitcast.39, bf16[2048,768]{1,0:T(8,128)(2,1)S(1)} %bitcast.41), kind=kOutput, calls=%fused_computation.4 | convolution fusion | flops 7262109696 | bytes 14548992 | tf_op jit(solution)/shard_map/dot_general | solution.py:195
  92.7 1.5 constant_dynamic-slice_fusion
  96.2 65.1 %gather_1.1 = bf16[16,128,2048]{2,1,0:T(8,128)(2,1)} custom-call(bf16[128,2048]{1,0:T(8,128)(2,1)} %refs_0_.2), custom_call_target="tpu_custom_call" | custom-call | tf_op jit(solution)/shard_map/gather_1/pallas_call | solution.py:121
  161.3 4.8 %convolution_convert_fusion.3 = bf16[16,72,2048]{2,1,0:T(8,128)(2,1)S(1)} fusion(bf16[16,128,2048]{2,1,0:T(8,128)(2,1)} %gather_1.1, s32[16,128]{1,0:T(8,128)S(1)} %fusion.23), kind=kOutput, calls=%fused_computation.15 | convolution fusion | flops 606486528 | bytes 13115392 | tf_op jit(solution)/shard_map/sct,std->scd/dot_general | solution.py:181
  166.1 3.9 %convolution_convert_fusion.7 = bf16[1152,768]{1,0:T(8,128)(2,1)S(1)} fusion(bf16[1152,2048]{1,0:T(8,128)(2,1)S(1)} %bitcast.35, bf16[1,768,2048]{2,1,0:T(8,128)(2,1)S(1)} %copy-done), kind=kOutput, calls=%fused_computation.21 | convolution fusion | flops 3624763392 | bytes 9633792 | tf_op jit(solution)/shard_map/dot_general | solution.py:208
  171.8 2.6 add_convert_fusion
  174.4 18.5 %collective-permute-done = bf16[576,768]{1,0:T(8,128)(2,1)S(1)} collective-permute-done((bf16[576,768]{1,0:T(8,128)(2,1)}, bf16[576,768]{1,0:T(8,128)(2,1)S(1)}, u32[]{:S(2)}, u32[]{:S(2)}) %collective-permute-start) | collective-permute-done | bytes 884768 | tf_op jit(solution)/shard_map/ppermute | solution.py:141
  192.9 1.7 multiply_reduce_fusion
  194.8 2.2 collective-permute-done.3
  197.9 2.5 fusion.9
  207.1 33.9 %collective-permute-done.2 = bf16[576,1536]{1,0:T(8,128)(2,1)} collective-permute-done((bf16[576,1536]{1,0:T(8,128)(2,1)}, bf16[576,1536]{1,0:T(8,128)(2,1)}, u32[]{:S(2)}, u32[]{:S(2)}) %collective-permute-start.2) | collective-permute-done | bytes 1769504 | tf_op jit(solution)/shard_map/ppermute | solution.py:141
  241.1 2.1 broadcast_select_fusion.1
  243.2 8.1 %convolution_convert_fusion.1 = bf16[1152,2048]{1,0:T(8,128)(2,1)S(1)} fusion(bf16[2048,768]{1,0:T(8,128)(2,1)S(1)} %bitcast.40, bf16[2048,768]{1,0:T(8,128)(2,1)S(1)} %bitcast.42, bf16[576,1536]{1,0:T(8,128)(2,1)S(1)} %get-tuple-element.22, bf16[576,1536]{1,0:T(8,128)(2,1)S(1)} %get-tuple-element.21), kind=kOutput, calls=%fused_computation.5 | convolution fusion | flops 7269777408 | bytes 14548992 | tf_op jit(solution)/shard_map/dot_general | solution.py:218
  251.3 5.7 %convolution_convert_fusion.2 = bf16[16,128,2048]{2,1,0:T(8,128)(2,1)} fusion(bf16[16,72,2048]{2,1,0:T(8,128)(2,1)S(1)} %bitcast.37, s32[16,128]{1,0:T(8,128)S(1)} %fusion.23), kind=kOutput, calls=%fused_computation.7 | convolution fusion | flops 608321536 | bytes 13115392 | tf_op jit(solution)/shard_map/sct,scd->std/dot_general | solution.py:222
  257.0 8.2 %gather_fusion = bf16[16,128,2048]{2,1,0:T(8,128)(2,1)} fusion(bf16[16,128,2048]{2,1,0:T(8,128)(2,1)} %convolution_convert_fusion.2, s32[1024]{0:T(1024)S(1)} %pad_clamp_fusion), kind=kCustom, calls=%fused_computation | custom fusion | bytes 16777280 | tf_op jit(solution)/shard_map/jit(_take)/gather | solution.py:240
  265.2 7.5 %bitcast_select_fusion = bf16[2048,2048]{1,0:T(8,128)(2,1)} fusion(bf16[16,128,2048]{2,1,0:T(8,128)(2,1)} %gather_fusion, pred[2048]{0:T(1024)(128)(4,1)S(1)} %broadcast_bitcast_fusion), kind=kLoop, calls=%fused_computation.3 | loop fusion | flops 4194304 | bytes 16779264 | tf_op jit(solution)/shard_map/jit(_take)/select_n | solution.py:240
  275.5 16.6 %collective-permute-done.4 = bf16[576,768]{1,0:T(8,128)(2,1)S(1)} collective-permute-done((bf16[576,768]{1,0:T(8,128)(2,1)S(1)}, bf16[576,768]{1,0:T(8,128)(2,1)S(1)}, u32[]{:S(2)}, u32[]{:S(2)}) %collective-permute-start.4) | collective-permute-done | bytes 884768 | tf_op jit(solution)/shard_map/ppermute | solution.py:141
  292.2 9.0 %fusion.6 = bf16[1,768,2048]{2,1,0:T(8,128)(2,1)} fusion(bf16[1152,2048]{1,0:T(8,128)(2,1)} %bitcast.36, f32[1152]{0:T(1024)S(1)} %reshape.78, bf16[576,768]{1,0:T(8,128)(2,1)S(1)} %get-tuple-element.24, bf16[576,768]{1,0:T(8,128)(2,1)S(1)} %get-tuple-element.23), kind=kOutput, calls=%fused_computation.25 | convolution fusion | flops 3636068352 | bytes 9638400 | tf_op jit(solution)/shard_map/dot_general | solution.py:246
  301.2 5.8 %fusion.4 = bf16[1,2048,768]{2,1,0:T(8,128)(2,1)} fusion(bf16[1152,2048]{1,0:T(8,128)(2,1)S(1)} %bitcast.33, bf16[576,1536]{1,0:T(8,128)(2,1)S(1)} %copy-done.12, bf16[576,1536]{1,0:T(8,128)(2,1)S(1)} %copy-done.14), kind=kOutput, calls=%fused_computation.23 | convolution fusion | flops 3628990464 | bytes 11403264 | tf_op jit(solution)/shard_map/dot_general | solution.py:249
  307.0 5.8 %fusion.5 = bf16[1,2048,768]{2,1,0:T(8,128)(2,1)} fusion(bf16[1152,2048]{1,0:T(8,128)(2,1)S(1)} %bitcast.34, bf16[576,1536]{1,0:T(8,128)(2,1)S(1)} %copy-done.12, bf16[576,1536]{1,0:T(8,128)(2,1)S(1)} %copy-done.14), kind=kOutput, calls=%fused_computation.24 | convolution fusion | flops 3628990464 | bytes 11403264 | tf_op jit(solution)/shard_map/dot_general | solution.py:252
  312.8 65.0 %reduce-scatter.5.cloned.1.call-done = bf16[128,2048]{1,0:T(8,128)(2,1)} async-done(((bf16[2048,2048]{1,0:T(8,128)(2,1)}), bf16[128,2048]{1,0:T(8,128)(2,1)}) %reduce-scatter.5.cloned.1.call-update) | async-done | bytes 524304 | tf_op jit(solution)/shard_map/reduce_scatter | solution.py:243
  (80 shorter events, 17.7 us)
Async XLA Ops:
  7.2 159.0 %copy-start = (bf16[1,768,2048]{2,1,0:T(8,128)(2,1)S(1)}, bf16[1,768,2048]{2,1,0:T(8,128)(2,1)}, u32[]{:S(2)}) copy-start(bf16[1,768,2048]{2,1,0:T(8,128)(2,1)} %param.13) | copy-start | bytes 9437188
  7.2 266.9 %reduce-scatter.7.cloned.1.call-start = ((), (), s32[]{:S(2)}) async-start(), calls=%async_computation.3 | async-start | bytes 557056
  79.3 4.9 %copy-start.15 = (bf16[1,2048,768]{2,1,0:T(8,128)(2,1)S(1)}, bf16[1,2048,768]{2,1,0:T(8,128)(2,1)}, u32[]{:S(2)}) copy-start(bf16[1,2048,768]{2,1,0:T(8,128)(2,1)} %param.12) | copy-start | bytes 9437188
  79.3 5.2 %copy-start.17 = (bf16[1,2048,768]{2,1,0:T(8,128)(2,1)S(1)}, bf16[1,2048,768]{2,1,0:T(8,128)(2,1)}, u32[]{:S(2)}) copy-start(bf16[1,2048,768]{2,1,0:T(8,128)(2,1)} %param.11) | copy-start | bytes 9437188
  84.2 8.4 %copy-start.2 = (bf16[16,72,2048]{2,1,0:T(8,128)(2,1)}, bf16[16,72,2048]{2,1,0:T(8,128)(2,1)S(1)}, u32[]{:S(2)}) copy-start(bf16[16,72,2048]{2,1,0:T(8,128)(2,1)S(1)} %convolution_convert_fusion.4) | copy-start | bytes 14155780
  95.0 76.8 %collective-permute-start.1 = (bf16[576,1536]{1,0:T(8,128)(2,1)}, bf16[576,1536]{1,0:T(8,128)(2,1)}, u32[]{:S(2)}, u32[]{:S(2)}) collective-permute-start(bf16[576,1536]{1,0:T(8,128)(2,1)} %constant_dynamic-slice_fusion), channel_id=1, source_target_pairs={{0,1},{1,0},{2,3},{3,2},{4,5},{5,4},{6,7},{7,6},{8,9},{9,8},{10,11... | collective-permute-start | bytes 5308424 | tf_op jit(solution)/shard_map/ppermute | solution.py:141
  166.1 3.9 %copy-start.3 = (bf16[16,72,2048]{2,1,0:T(8,128)(2,1)}, bf16[16,72,2048]{2,1,0:T(8,128)(2,1)S(1)}, u32[]{:S(2)}) copy-start(bf16[16,72,2048]{2,1,0:T(8,128)(2,1)S(1)} %convolution_convert_fusion.3) | copy-start | bytes 14155780
  171.5 21.3 %collective-permute-start = (bf16[576,768]{1,0:T(8,128)(2,1)}, bf16[576,768]{1,0:T(8,128)(2,1)S(1)}, u32[]{:S(2)}, u32[]{:S(2)}) collective-permute-start(bf16[576,768]{1,0:T(8,128)(2,1)} %constant_dynamic-slice_fusion.1), channel_id=1, source_target_pairs={{0,1},{1,0},{2,3},{3,2},{4,5},{5,4},{6,7},{7,6},{8,9},{9,8},{10,11... | collective-permute-start | bytes 2654216 | tf_op jit(solution)/shard_map/ppermute | solution.py:141
  171.8 21.1 %copy-start.7 = (bf16[1152,768]{1,0:T(8,128)(2,1)S(1)}, bf16[1152,768]{1,0:T(8,128)(2,1)}, u32[]{:S(2)}) copy-start(bf16[1152,768]{1,0:T(8,128)(2,1)} %copy-done.6) | copy-start | bytes 5308420
  192.9 4.9 %copy-start.9 = (bf16[576,768]{1,0:T(8,128)(2,1)}, bf16[576,768]{1,0:T(8,128)(2,1)S(1)}, u32[]{:S(2)}) copy-start(bf16[576,768]{1,0:T(8,128)(2,1)S(1)} %collective-permute-done) | copy-start | bytes 2654212
  194.5 2.4 collective-permute-start.3
  202.7 38.4 %copy-start.5 = (bf16[576,768]{1,0:T(8,128)(2,1)S(1)}, bf16[576,768]{1,0:T(8,128)(2,1)}, u32[]{:S(2)}) copy-start(bf16[576,768]{1,0:T(8,128)(2,1)} %copy-done.4) | copy-start | bytes 2654212
  202.7 38.4 %collective-permute-start.2 = (bf16[576,1536]{1,0:T(8,128)(2,1)}, bf16[576,1536]{1,0:T(8,128)(2,1)}, u32[]{:S(2)}, u32[]{:S(2)}) collective-permute-start(bf16[576,1536]{1,0:T(8,128)(2,1)} %pad_maximum_fusion.5), channel_id=1, source_target_pairs={{0,1},{1,0},{2,3},{3,2},{4,5},{5,4},{6,7},{7,6},{8,9},{9,8},{10,11... | collective-permute-start | bytes 5308424 | tf_op jit(solution)/shard_map/ppermute | solution.py:141
  207.0 170.8 %reduce-scatter.5.cloned.1.call-start = ((), (), s32[]{:S(2)}) async-start(), calls=%async_computation.2 | async-start | bytes 8912896 | tf_op jit(solution)/shard_map/reduce_scatter | solution.py:243
  207.1 36.1 %copy-start.16 = (bf16[1,2048,768]{2,1,0:T(8,128)(2,1)S(1)}, bf16[1,2048,768]{2,1,0:T(8,128)(2,1)}, u32[]{:S(2)}) copy-start(bf16[1,2048,768]{2,1,0:T(8,128)(2,1)} %param.12) | copy-start | bytes 9437188
  207.1 36.1 %copy-start.18 = (bf16[1,2048,768]{2,1,0:T(8,128)(2,1)S(1)}, bf16[1,2048,768]{2,1,0:T(8,128)(2,1)}, u32[]{:S(2)}) copy-start(bf16[1,2048,768]{2,1,0:T(8,128)(2,1)} %param.11) | copy-start | bytes 9437188
  243.2 8.1 %copy-start.11 = (bf16[576,1536]{1,0:T(8,128)(2,1)}, bf16[576,1536]{1,0:T(8,128)(2,1)S(1)}, u32[]{:S(2)}) copy-start(bf16[576,1536]{1,0:T(8,128)(2,1)S(1)} %get-tuple-element.21) | copy-start | bytes 5308420
  243.2 8.1 %copy-start.13 = (bf16[576,1536]{1,0:T(8,128)(2,1)}, bf16[576,1536]{1,0:T(8,128)(2,1)S(1)}, u32[]{:S(2)}) copy-start(bf16[576,1536]{1,0:T(8,128)(2,1)S(1)} %get-tuple-element.22) | copy-start | bytes 5308420
  273.8 18.2 %collective-permute-start.4 = (bf16[576,768]{1,0:T(8,128)(2,1)S(1)}, bf16[576,768]{1,0:T(8,128)(2,1)S(1)}, u32[]{:S(2)}, u32[]{:S(2)}) collective-permute-start(bf16[576,768]{1,0:T(8,128)(2,1)S(1)} %copy-done.10), channel_id=1, source_target_pairs={{0,1},{1,0},{2,3},{3,2},{4,5},{5,4},{6,7},{7,6},{8,9},{9,8},{10,11... | collective-permute-start | bytes 2654216 | tf_op jit(solution)/shard_map/ppermute | solution.py:141
  292.1 9.1 %slice-start = ((s8[4718592]{0:T(1024)(128)(4,1)}), s8[4194304]{0:T(1024)(128)(4,1)S(1)}, s32[]{:S(2)}) async-start(s8[4718592]{0:T(1024)(128)(4,1)} %bitcast.31), calls=%async_computation.4 | async-start | bytes 8388608
  292.2 9.0 %slice-start.1 = ((s8[4718592]{0:T(1024)(128)(4,1)}), s8[524288]{0:T(1024)(128)(4,1)S(1)}, s32[]{:S(2)}) async-start(s8[4718592]{0:T(1024)(128)(4,1)} %bitcast.31), calls=%async_computation.5 | async-start | bytes 1048576
  292.2 9.0 %copy-start.12 = (bf16[576,1536]{1,0:T(8,128)(2,1)S(1)}, bf16[576,1536]{1,0:T(8,128)(2,1)}, u32[]{:S(2)}) copy-start(bf16[576,1536]{1,0:T(8,128)(2,1)} %copy-done.11) | copy-start | bytes 5308420
  292.2 9.0 %copy-start.14 = (bf16[576,1536]{1,0:T(8,128)(2,1)S(1)}, bf16[576,1536]{1,0:T(8,128)(2,1)}, u32[]{:S(2)}) copy-start(bf16[576,1536]{1,0:T(8,128)(2,1)} %copy-done.13) | copy-start | bytes 5308420
  307.0 70.8 %copy-start.1 = (bf16[1,768,2048]{2,1,0:T(8,128)(2,1)S(1)}, bf16[1,768,2048]{2,1,0:T(8,128)(2,1)}, u32[]{:S(2)}) copy-start(bf16[1,768,2048]{2,1,0:T(8,128)(2,1)} %param.13) | copy-start | bytes 9437188
  (4 other events, 5.9 us)
Sparse Core Ops, SparseCore 0:
  207.2 55.9 reduce-scatter.6
  272.8 104.9 reduce-scatter.4
